TPU v7x, 256 devices: a whole 4x4x8 slice. The times are simulated.
256 devices in a mesh: tp: 2 (over z_lo), sp: 32 (over x, y, core), dp: 4 (over z_hi).
Axes of the slice: x: 4, y: 4, z: 8 (z_hi: 4, z_lo: 2; z = z_hi * 2 + z_lo), core: 2. Of those that a mesh axis runs over, the one named last changes fastest.
Arguments:
- queries: bfloat16 [16384, 4096], P(('dp', 'sp'), 'tp'), parts along dimension 0, may hold values from -256 to 256
- key_projection_rows: bfloat16 [16384, 512], P(('dp', 'sp'), 'tp'), parts along dimension 0, may hold values from -8 to 8
- values: bfloat16 [16384, 512], P(('dp', 'sp'), 'tp'), parts along dimension 0, may hold values from -6 to 6
- segment_ids: int32 [16384], P('dp'), parts along dimension 0, may hold values from 0 to 11, never falling along the last dimension, each value on 1 to 1024 neighbouring positions
- residual: bfloat16 [16384, 8192], P(('dp', 'tp'), 'sp'), parts along dimension 0, may hold values from -40 to 40
- out_weight: bfloat16 [4096, 8192], P('tp', 'sp'), may hold values from -0.09375 to 0.09375
- norm_gain: float32 [8192], P('sp'), may hold values from 0.1 to 1.9
- scale_exponent: int32 [8192], P('sp'), may hold values from 7 to 8
Outputs:
- hidden_out: bfloat16 [16384, 8192], P(('dp', 'tp'), 'sp'), parts along dimension 0
- quantized: bfloat16 [16384, 8192], P(('dp', 'tp'), 'sp'), parts along dimension 0
There are 4 independent parts, one for each index of `dp`. A program takes and returns all parts, laid end to end along the dimension named above; an argument that names none is the same for every part. Nothing has to cross between parts.
Inputs may be any that keep to these rules, and one draw needn't show every extreme that they name: `segment_ids`: never falls along the window; every document holds at most a quarter of the window's tokens, and one holds exactly that many.
All inputs are finite; a program needn't handle non-finite values.
Results may differ from a plain program's by a relative error of at most 0.0065.
Values may be sent and summed in bfloat16 or wider, within the bound.
No kernel may reach another device: no remote copies, remote signals or barrier semaphores. Data moves between devices by JAX's collectives and lax.ppermute only.
A program may use at most 64 MiB of HBM per device.

v0:
```python
import jax
import jax.numpy as jnp
from jax import lax
from jax.sharding import PartitionSpec as P

D = 8192
QUERY_HEAD_COUNT = 32
KEY_VALUE_HEADS = 4
HEAD_DIMENSION = 128
epsilon = 1e-05
limit_value = 448.0


def attend_item(query_block, key_block, value_block, query_pos, query_seg, segment_ids, key_pos):
    query_count = query_block.shape[0]
    block_rows = min(512, query_count)
    blocks = query_count // block_rows

    def one_block(packed):
        block_query, block_pos, block_seg = packed
        scores = lax.dot_general(
            block_query, key_block, (((1,), (1,)), ((), ())), preferred_element_type=jnp.float32
        ) * HEAD_DIMENSION ** (-0.5)
        visible = (key_pos[None, :] <= block_pos[:, None]) & (
            segment_ids[None, :] == block_seg[:, None]
        )
        scores = jnp.where(visible, scores, -1e30)
        largest = jnp.max(scores, axis=1, keepdims=True)
        weights = jnp.exp(scores - largest)
        row_total = jnp.sum(weights, axis=1, keepdims=True)
        probabilities = (weights / row_total).astype(jnp.bfloat16)
        return jnp.dot(probabilities, value_block, preferred_element_type=jnp.float32).astype(
            jnp.bfloat16
        )

    results = lax.map(
        one_block,
        (
            query_block.reshape(blocks, block_rows, HEAD_DIMENSION),
            query_pos.reshape(blocks, block_rows),
            query_seg.reshape(blocks, block_rows),
        ),
    )
    return results.reshape(query_count, HEAD_DIMENSION)


def body(
    queries,
    key_projection_rows,
    values,
    segment_ids,
    residual,
    out_weight,
    norm_gain,
    scale_exponent,
):
    sp_count = lax.axis_size("sp")
    token_rows = queries.shape[0]
    half_rows = token_rows // 2
    local_heads = queries.shape[1] // HEAD_DIMENSION
    item_count = 2 * local_heads
    per_device = item_count // sp_count
    window_token_rows = token_rows * sp_count
    query_count = window_token_rows // 2
    group_width = QUERY_HEAD_COUNT // KEY_VALUE_HEADS
    own_index = lax.axis_index("sp")
    query_items = jnp.transpose(
        queries.reshape(2, half_rows, local_heads, HEAD_DIMENSION), (0, 2, 1, 3)
    ).reshape(item_count, half_rows, HEAD_DIMENSION)
    query_recv = lax.all_to_all(query_items, "sp", split_axis=0, concat_axis=1, tiled=True)
    key_all, value_all = (
        lax.all_gather(key_projection_rows, "sp", axis=0, tiled=True),
        lax.all_gather(values, "sp", axis=0, tiled=True),
    )
    key_pos = jnp.arange(window_token_rows, dtype=jnp.int32)
    row_number = jnp.arange(query_count, dtype=jnp.int32)
    source_device = row_number // half_rows
    within = row_number % half_rows
    segment_grid = segment_ids.reshape(sp_count, 2, half_rows)
    number = 0
    item_index = own_index * per_device + number
    which_half = item_index // local_heads
    query_pos = source_device * token_rows + which_half * half_rows + within
    query_seg = lax.dynamic_index_in_dim(segment_grid, which_half, 1, keepdims=False).reshape(
        query_count
    )
    shared_rows = item_index % local_heads // group_width
    key_block = lax.dynamic_slice_in_dim(key_all, shared_rows * HEAD_DIMENSION, HEAD_DIMENSION, 1)
    value_block = lax.dynamic_slice_in_dim(
        value_all, shared_rows * HEAD_DIMENSION, HEAD_DIMENSION, 1
    )
    outputs = [
        attend_item(
            query_recv[number], key_block, value_block, query_pos, query_seg, segment_ids, key_pos
        )
    ]
    own_outputs = jnp.stack(outputs)
    column_count = out_weight.shape[1]
    start_sum = jnp.zeros((sp_count, 2, half_rows, column_count), jnp.float32)
    pieces = lax.all_gather(own_outputs, "sp", axis=0, tiled=True)

    def add_one(number, current):
        head_number = number % local_heads
        which_half = number // local_heads
        head_weight = lax.dynamic_slice_in_dim(
            out_weight, head_number * HEAD_DIMENSION, HEAD_DIMENSION, 0
        )
        chosen = lax.dynamic_index_in_dim(pieces, number, 0, keepdims=False)
        product_term = jnp.dot(chosen, head_weight, preferred_element_type=jnp.float32).reshape(
            sp_count, 1, half_rows, column_count
        )
        corner = (0, which_half, 0, 0)
        earlier = lax.dynamic_slice(current, corner, (sp_count, 1, half_rows, column_count))
        return lax.dynamic_update_slice(current, earlier + product_term, corner)

    combined = lax.fori_loop(0, pieces.shape[0], add_one, start_sum)
    flattened = combined.reshape(window_token_rows, column_count)
    share_rows = window_token_rows // lax.axis_size("tp")
    whole_sum = lax.psum(flattened, "tp")
    summed = lax.dynamic_slice_in_dim(whole_sum, lax.axis_index("tp") * share_rows, share_rows, 0)
    projected = summed.astype(jnp.bfloat16)
    hidden_out = (residual.astype(jnp.float32) + projected.astype(jnp.float32)).astype(jnp.bfloat16)
    widened = hidden_out.astype(jnp.float32)
    square_sum = lax.psum(jnp.sum(widened * widened, axis=1), "sp")
    mean_square = (square_sum / D)[:, None]
    normed = widened * lax.rsqrt(mean_square + epsilon) * norm_gain[None, :]
    clip_bound = (limit_value * jnp.exp2(-scale_exponent.astype(jnp.float32)))[None, :]
    quantized = jnp.clip(normed, -clip_bound, clip_bound).astype(jnp.bfloat16)
    return (hidden_out, quantized)


def solution(mesh):
    in_specs = (
        P(("dp", "sp"), "tp"),
        P(("dp", "sp"), "tp"),
        P(("dp", "sp"), "tp"),
        P("dp"),
        P(("dp", "tp"), "sp"),
        P("tp", "sp"),
        P("sp"),
        P("sp"),
    )
    out_specs = (P(("dp", "tp"), "sp"), P(("dp", "tp"), "sp"))
    return jax.shard_map(body, mesh=mesh, in_specs=in_specs, out_specs=out_specs, check_vma=False)
```

profile of v0, /device:TPU:1, one launch (start us, length us, event | category | flops | bytes accessed | tf_op | source)
XLA Modules:
  0.0 569.2 jit_solution(7606608849317972235)
XLA Ops:
  10.8 8.6 %all-to-all-start = ((bf16[32,64,128]{2,1,0:T(8,128)(2,1)}), bf16[32,64,128]{2,1,0:T(8,128)(2,1)S(1)}, u32[]{:S(2)}, u32[]{:S(2)}) async-start(bf16[32,64,128]{2,1,0:T(8,128)(2,1)} %bitcast.4), calls=%async_computation | async-start | bytes 1048576 | tf_op jit(solution)/shard_map/all_to_all | solution.py:70
  19.8 43.6 %all-gather.6.cloned.1.call-done = bf16[4096,256]{1,0:T(8,128)(2,1)} async-done(((bf16[128,256]{1,0:T(8,128)(2,1)}), bf16[4096,256]{1,0:T(8,128)(2,1)}) %all-gather.6.cloned.1.call-update) | async-done | bytes 2097168 | tf_op jit(solution)/shard_map/all_gather | solution.py:73
  64.6 49.3 %all-gather.4.cloned.1.call-done = bf16[4096,256]{1,0:T(8,128)(2,1)} async-done(((bf16[128,256]{1,0:T(8,128)(2,1)}), bf16[4096,256]{1,0:T(8,128)(2,1)}) %all-gather.4.cloned.1.call-update) | async-done | bytes 2097168 | tf_op jit(solution)/shard_map/all_gather | solution.py:72
  115.2 24.3 %while.27 = (s32[]{:T(128)}, bf16[4,512,128]{2,1,0:T(8,128)(2,1)S(1)}, s32[4,512]{1,0:T(4,128)S(1)}, s32[4096]{0:T(1024)S(1)}, s32[4,512]{1,0:T(4,128)S(1)}, /*i...) while((s32[]{:T(128)}, ...), condition=%wide.region_3.4_spmd.clone, body=%wide.region_0.3_spmd.clone.sunk | while | flops 1096875008 | bytes 27564136 | solution.py:36
  115.2 2.5 fusion.40
  121.3 2.5 fusion.40
  125.1 2.2 fusion.42
  127.4 2.5 fusion.40
  131.2 2.2 fusion.42
  133.4 2.5 fusion.40
  137.2 2.2 fusion.42
  140.3 77.1 %all-gather.8.cloned.1.call-done = bf16[32,2048,128]{2,1,0:T(8,128)(2,1)} async-done(((bf16[1,2048,128]{2,1,0:T(8,128)(2,1)}), bf16[32,2048,128]{2,1,0:T(8,128)(2,1)}) %all-gather.8.cloned.1.call-update) | async-done | bytes 16777232 | tf_op jit(solution)/shard_map/all_gather | solution.py:100
  217.4 2.4 broadcast_in_dim.18.clone
  219.9 174.8 %while.26 = (s32[]{:T(128)}, f32[32,2,64,256]{3,2,1,0:T(8,128)}, bf16[32,2048,128]{2,1,0:T(8,128)(2,1)}, bf16[2048,256]{1,0:T(8,128)(2,1)}, s32[]{:T(128)}, /*in...) while((s32[]{:T(128)}, f32[32,2,64,256]{3,2,1,0:T(8,128)}, ...), condition=%wide.region_5.6_spmd, body=%wide.region_4.5_spmd.sunk | while | flops 134742032 | bytes 10027344 | solution.py:116
  222.7 2.6 bitcast_dynamic-update-slice_fusion.2
  228.1 2.6 bitcast_dynamic-update-slice_fusion.2
  233.6 2.6 bitcast_dynamic-update-slice_fusion.2
  239.0 2.6 bitcast_dynamic-update-slice_fusion.2
  244.4 2.6 bitcast_dynamic-update-slice_fusion.2
  249.9 2.6 bitcast_dynamic-update-slice_fusion.2
  255.3 2.6 bitcast_dynamic-update-slice_fusion.2
  260.7 2.6 bitcast_dynamic-update-slice_fusion.2
  266.1 2.6 bitcast_dynamic-update-slice_fusion.2
  271.6 2.6 bitcast_dynamic-update-slice_fusion.2
  277.0 2.6 bitcast_dynamic-update-slice_fusion.2
  282.4 2.6 bitcast_dynamic-update-slice_fusion.2
  287.9 2.6 bitcast_dynamic-update-slice_fusion.2
  293.3 2.6 bitcast_dynamic-update-slice_fusion.2
  298.7 2.6 bitcast_dynamic-update-slice_fusion.2
  304.1 2.6 bitcast_dynamic-update-slice_fusion.2
  309.6 2.6 bitcast_dynamic-update-slice_fusion.2
  315.1 2.6 bitcast_dynamic-update-slice_fusion.2
  320.6 2.6 bitcast_dynamic-update-slice_fusion.2
  326.0 2.6 bitcast_dynamic-update-slice_fusion.2
  331.5 2.6 bitcast_dynamic-update-slice_fusion.2
  337.0 2.6 bitcast_dynamic-update-slice_fusion.2
  342.5 2.6 bitcast_dynamic-update-slice_fusion.2
  348.0 2.6 bitcast_dynamic-update-slice_fusion.2
  353.5 2.6 bitcast_dynamic-update-slice_fusion.2
  359.0 2.6 bitcast_dynamic-update-slice_fusion.2
  364.5 2.6 bitcast_dynamic-update-slice_fusion.2
  370.0 2.6 bitcast_dynamic-update-slice_fusion.2
  375.5 2.6 bitcast_dynamic-update-slice_fusion.2
  381.0 2.6 bitcast_dynamic-update-slice_fusion.2
  386.5 2.6 bitcast_dynamic-update-slice_fusion.2
  392.0 2.6 bitcast_dynamic-update-slice_fusion.2
  394.7 100.2 %all-reduce.1 = bf16[4096,256]{1,0:T(8,128)(2,1)S(1)} all-reduce(f32[4096,256]{1,0:T(8,128)} %bitcast.61), channel_id=1, replica_groups=mesh['tp'=2,'sp'=32,'dp'=4] {'tp'}, use_global_device_ids=true, to_apply=%region_6.7 | all-reduce | flops 1048576 | bytes 6291456 | tf_op jit(solution)/shard_map/psum | solution.py:119
  496.6 64.7 %psum.15 = f32[2048]{0:T(1024)S(1)} all-reduce(f32[2048]{0:T(1024)S(1)} %get-tuple-element.206), channel_id=1, replica_groups=mesh['tp'=2,'sp'=32,'dp'=4] {'sp'}, use_global_device_ids=true, to_apply=%region_8.9 | all-reduce | flops 2048 | bytes 16384 | tf_op jit(solution)/shard_map/psum | solution.py:124
  (104 shorter events, 108.5 us)
Async XLA Ops:
  7.2 12.3 %copy-start.2 = (s32[4096]{0:T(1024)S(1)}, s32[4096]{0:T(1024)}, u32[]{:S(2)}) copy-start(s32[4096]{0:T(1024)} %param.15) | copy-start | bytes 49156
  7.2 56.2 %all-gather.6.cloned.1.call-start = ((), (), s32[]{:S(2)}) async-start(), calls=%async_computation.2 | async-start | bytes 2162688 | tf_op jit(solution)/shard_map/all_gather | solution.py:73
  7.9 106.0 %all-gather.4.cloned.1.call-start = ((), (), s32[]{:S(2)}) async-start(), calls=%async_computation.1 | async-start | bytes 2162688 | tf_op jit(solution)/shard_map/all_gather | solution.py:72
  10.8 104.4 %all-to-all-start = ((bf16[32,64,128]{2,1,0:T(8,128)(2,1)}), bf16[32,64,128]{2,1,0:T(8,128)(2,1)S(1)}, u32[]{:S(2)}, u32[]{:S(2)}) async-start(bf16[32,64,128]{2,1,0:T(8,128)(2,1)} %bitcast.4), calls=%async_computation | async-start | bytes 1048576 | tf_op jit(solution)/shard_map/all_to_all | solution.py:70
  19.4 198.0 %all-gather.8.cloned.1.call-start = ((), (), s32[]{:S(2)}) async-start(), calls=%async_computation.3 | async-start | bytes 17301504 | tf_op jit(solution)/shard_map/all_gather | solution.py:100
  115.2 25.1 %copy-start.4 = (s32[256]{0:T(256)S(1)}, s32[256]{0:T(256)}, u32[]{:S(2)}) copy-start(s32[256]{0:T(256)} %param.19) | copy-start | bytes 3076
  139.5 0.8 copy-start.1
  394.7 166.6 %copy-start.3 = (f32[256]{0:T(256)S(1)}, f32[256]{0:T(256)}, u32[]{:S(2)}) copy-start(f32[256]{0:T(256)} %param.18) | copy-start | bytes 3076
  496.5 66.2 %copy-start = (bf16[2048,256]{1,0:T(8,128)(2,1)}, bf16[2048,256]{1,0:T(8,128)(2,1)S(1)}, u32[]{:S(2)}) copy-start(bf16[2048,256]{1,0:T(8,128)(2,1)S(1)} %get-tuple-element.207) | copy-start | bytes 3145732
Sparse Core Ops, SparseCore 0:
  10.5 52.7 all-gather.5
  65.9 47.9 all-gather.3
  140.4 76.9 all-gather.7
where the time goes:
time: 574 us; the launch traced here: 569 us
  waiting for transfers between devices  171 us (30%)
  blocking collectives  165 us (29%)
  matrix products  103 us (18%)
  local copies, waits for them, and re-layouts  98.9 us (17%)
  between operations  14 us (2%)
  starting transfers between devices  8.69 us (2%)
  other arithmetic  8.28 us (1%)
    psum x1, blocking collectives, body(): whole_sum = lax.psum(flattened, 'tp')  100 us
    dot_general x32, matrix products, add_one(): jnp.dot(chosen, head_weight, preferred_element_type=jnp.float32)  83.6 us
    all_gather x1, waiting for transfers between devices, body(): pieces = lax.all_gather(own_outputs, 'sp', axis=0, tiled=True)  77.1 us
    psum x1, blocking collectives, body(): square_sum = lax.psum(jnp.sum(widened * widened, axis=1), 'sp')  64.7 us
    dynamic_slice x32, local copies, waits for them, and re-layouts, add_one(): lax.dynamic_slice(current, corner, (sp_count, 1, half_rows, column_count))  56.2 us
    all_gather x1, waiting for transfers between devices, body(): lax.all_gather(key_projection_rows, 'sp', axis=0, tiled=True)  49.3 us
    all_gather x1, waiting for transfers between devices, body(): lax.all_gather(values, 'sp', axis=0, tiled=True)  43.6 us
    dynamic_slice x32, local copies, waits for them, and re-layouts, add_one(): chosen = lax.dynamic_index_in_dim(pieces, number, 0, keepdims=False)  34.6 us
  transfers between devices with their start and end apart: 4, of which 3 were waited for; matrix products, arithmetic and copies ran while one was open for 1% of the time, Pallas kernels for 0%

commit v1 on v0

--- a/solution.py
+++ b/solution.py
@@ -121,7 +121,7 @@
     projected = summed.astype(jnp.bfloat16)
     hidden_out = (residual.astype(jnp.float32) + projected.astype(jnp.float32)).astype(jnp.bfloat16)
     widened = hidden_out.astype(jnp.float32)
-    square_sum = lax.psum(jnp.sum(widened * widened, axis=1), "sp")
+    square_sum = jnp.sum(lax.all_gather(jnp.sum(widened * widened, axis=1), "sp"), axis=0)
     mean_square = (square_sum / D)[:, None]
     normed = widened * lax.rsqrt(mean_square + epsilon) * norm_gain[None, :]
     clip_bound = (limit_value * jnp.exp2(-scale_exponent.astype(jnp.float32)))[None, :]

time: 574 us -> 535 us (0.932)
  blocking collectives: 165 us -> 126 us
    psum x1 -> x0, blocking collectives: 64.7 us -> none  [body(): square_sum = lax.psum(jnp.sum(widened * widened, axis=1), 'sp')]
    all_gather x0 -> x1, blocking collectives: none -> 26.1 us  [body(): lax.all_gather(jnp.sum(widened * widened, axis=1), 'sp')]
where the time goes in v1:
time: 535 us; the launch traced here: 531 us
  waiting for transfers between devices  171 us (32%)
  blocking collectives  126 us (24%)
  matrix products  103 us (19%)
  local copies, waits for them, and re-layouts  99 us (19%)
  between operations  14 us (3%)
  starting transfers between devices  8.69 us (2%)
  other arithmetic  8.31 us (2%)
    psum x1, blocking collectives, body(): whole_sum = lax.psum(flattened, 'tp')  100 us
    dot_general x32, matrix products, add_one(): jnp.dot(chosen, head_weight, preferred_element_type=jnp.float32)  83.6 us
    all_gather x1, waiting for transfers between devices, body(): pieces = lax.all_gather(own_outputs, 'sp', axis=0, tiled=True)  77.1 us
    dynamic_slice x32, local copies, waits for them, and re-layouts, add_one(): lax.dynamic_slice(current, corner, (sp_count, 1, half_rows, column_count))  56.2 us
    all_gather x1, waiting for transfers between devices, body(): lax.all_gather(key_projection_rows, 'sp', axis=0, tiled=True)  49.3 us
    all_gather x1, waiting for transfers between devices, body(): lax.all_gather(values, 'sp', axis=0, tiled=True)  43.6 us
    dynamic_slice x32, local copies, waits for them, and re-layouts, add_one(): chosen = lax.dynamic_index_in_dim(pieces, number, 0, keepdims=False)  34.6 us
    all_gather x1, blocking collectives, body(): lax.all_gather(jnp.sum(widened * widened, axis=1), 'sp')  26.1 us
  transfers between devices with their start and end apart: 4, of which 3 were waited for; matrix products, arithmetic and copies ran while one was open for 1% of the time, Pallas kernels for 0%

profile of v1, /device:TPU:1, one launch (start us, length us, event | category | flops | bytes accessed | tf_op | source)
XLA Modules:
  0.0 530.7 jit_solution(12649606617888664016)
XLA Ops:
  10.8 8.6 %all-to-all-start = ((bf16[32,64,128]{2,1,0:T(8,128)(2,1)}), bf16[32,64,128]{2,1,0:T(8,128)(2,1)S(1)}, u32[]{:S(2)}, u32[]{:S(2)}) async-start(bf16[32,64,128]{2,1,0:T(8,128)(2,1)} %bitcast.4), calls=%async_computation | async-start | bytes 1048576 | tf_op jit(solution)/shard_map/all_to_all | solution.py:70
  19.8 43.6 %all-gather.7.cloned.1.call-done = bf16[4096,256]{1,0:T(8,128)(2,1)} async-done(((bf16[128,256]{1,0:T(8,128)(2,1)}), bf16[4096,256]{1,0:T(8,128)(2,1)}) %all-gather.7.cloned.1.call-update) | async-done | bytes 2097168 | tf_op jit(solution)/shard_map/all_gather | solution.py:73
  64.6 49.3 %all-gather.5.cloned.1.call-done = bf16[4096,256]{1,0:T(8,128)(2,1)} async-done(((bf16[128,256]{1,0:T(8,128)(2,1)}), bf16[4096,256]{1,0:T(8,128)(2,1)}) %all-gather.5.cloned.1.call-update) | async-done | bytes 2097168 | tf_op jit(solution)/shard_map/all_gather | solution.py:72
  115.2 24.3 %while.27 = (s32[]{:T(128)}, bf16[4,512,128]{2,1,0:T(8,128)(2,1)S(1)}, s32[4,512]{1,0:T(4,128)S(1)}, s32[4096]{0:T(1024)S(1)}, s32[4,512]{1,0:T(4,128)S(1)}, /*i...) while((s32[]{:T(128)}, ...), condition=%wide.region_3.4_spmd.clone, body=%wide.region_0.3_spmd.clone.sunk | while | flops 1096875008 | bytes 27564136 | solution.py:36
  115.2 2.5 fusion.40
  121.3 2.5 fusion.40
  125.1 2.2 fusion.42
  127.4 2.5 fusion.40
  131.2 2.2 fusion.42
  133.4 2.5 fusion.40
  137.2 2.2 fusion.42
  140.3 77.1 %all-gather.9.cloned.1.call-done = bf16[32,2048,128]{2,1,0:T(8,128)(2,1)} async-done(((bf16[1,2048,128]{2,1,0:T(8,128)(2,1)}), bf16[32,2048,128]{2,1,0:T(8,128)(2,1)}) %all-gather.9.cloned.1.call-update) | async-done | bytes 16777232 | tf_op jit(solution)/shard_map/all_gather | solution.py:100
  217.4 2.4 broadcast_in_dim.18.clone
  219.9 174.8 %while.26 = (s32[]{:T(128)}, f32[32,2,64,256]{3,2,1,0:T(8,128)}, bf16[32,2048,128]{2,1,0:T(8,128)(2,1)}, bf16[2048,256]{1,0:T(8,128)(2,1)}, s32[]{:T(128)}, /*in...) while((s32[]{:T(128)}, f32[32,2,64,256]{3,2,1,0:T(8,128)}, ...), condition=%wide.region_5.6_spmd, body=%wide.region_4.5_spmd.sunk | while | flops 134742032 | bytes 10027344 | solution.py:116
  222.7 2.6 bitcast_dynamic-update-slice_fusion.2
  228.1 2.6 bitcast_dynamic-update-slice_fusion.2
  233.6 2.6 bitcast_dynamic-update-slice_fusion.2
  239.0 2.6 bitcast_dynamic-update-slice_fusion.2
  244.4 2.6 bitcast_dynamic-update-slice_fusion.2
  249.9 2.6 bitcast_dynamic-update-slice_fusion.2
  255.3 2.6 bitcast_dynamic-update-slice_fusion.2
  260.7 2.6 bitcast_dynamic-update-slice_fusion.2
  266.1 2.6 bitcast_dynamic-update-slice_fusion.2
  271.6 2.6 bitcast_dynamic-update-slice_fusion.2
  277.0 2.6 bitcast_dynamic-update-slice_fusion.2
  282.4 2.6 bitcast_dynamic-update-slice_fusion.2
  287.9 2.6 bitcast_dynamic-update-slice_fusion.2
  293.3 2.6 bitcast_dynamic-update-slice_fusion.2
  298.7 2.6 bitcast_dynamic-update-slice_fusion.2
  304.1 2.6 bitcast_dynamic-update-slice_fusion.2
  309.6 2.6 bitcast_dynamic-update-slice_fusion.2
  315.1 2.6 bitcast_dynamic-update-slice_fusion.2
  320.6 2.6 bitcast_dynamic-update-slice_fusion.2
  326.0 2.6 bitcast_dynamic-update-slice_fusion.2
  331.5 2.6 bitcast_dynamic-update-slice_fusion.2
  337.0 2.6 bitcast_dynamic-update-slice_fusion.2
  342.5 2.6 bitcast_dynamic-update-slice_fusion.2
  348.0 2.6 bitcast_dynamic-update-slice_fusion.2
  353.5 2.6 bitcast_dynamic-update-slice_fusion.2
  359.0 2.6 bitcast_dynamic-update-slice_fusion.2
  364.5 2.6 bitcast_dynamic-update-slice_fusion.2
  370.0 2.6 bitcast_dynamic-update-slice_fusion.2
  375.5 2.6 bitcast_dynamic-update-slice_fusion.2
  381.0 2.6 bitcast_dynamic-update-slice_fusion.2
  386.5 2.6 bitcast_dynamic-update-slice_fusion.2
  392.0 2.6 bitcast_dynamic-update-slice_fusion.2
  394.7 100.2 %all-reduce.1 = bf16[4096,256]{1,0:T(8,128)(2,1)S(1)} all-reduce(f32[4096,256]{1,0:T(8,128)} %bitcast.61), channel_id=1, replica_groups=mesh['tp'=2,'sp'=32,'dp'=4] {'tp'}, use_global_device_ids=true, to_apply=%region_6.7 | all-reduce | flops 1048576 | bytes 6291456 | tf_op jit(solution)/shard_map/psum | solution.py:119
  496.6 26.1 %all-gather = f32[65536]{0:T(1024)S(1)} all-gather(f32[2048]{0:T(1024)S(1)} %get-tuple-element.206), channel_id=2, replica_groups=mesh['tp'=2,'sp'=32,'dp'=4] {'sp'}, dimensions={0}, use_global_device_ids=true | all-gather | bytes 270336 | tf_op jit(solution)/shard_map/all_gather | solution.py:124
  (106 shorter events, 108.6 us)
Async XLA Ops:
  7.2 12.3 %copy-start.2 = (s32[4096]{0:T(1024)S(1)}, s32[4096]{0:T(1024)}, u32[]{:S(2)}) copy-start(s32[4096]{0:T(1024)} %param.15) | copy-start | bytes 49156
  7.2 56.2 %all-gather.7.cloned.1.call-start = ((), (), s32[]{:S(2)}) async-start(), calls=%async_computation.2 | async-start | bytes 2162688 | tf_op jit(solution)/shard_map/all_gather | solution.py:73
  7.9 106.0 %all-gather.5.cloned.1.call-start = ((), (), s32[]{:S(2)}) async-start(), calls=%async_computation.1 | async-start | bytes 2162688 | tf_op jit(solution)/shard_map/all_gather | solution.py:72
  10.8 104.4 %all-to-all-start = ((bf16[32,64,128]{2,1,0:T(8,128)(2,1)}), bf16[32,64,128]{2,1,0:T(8,128)(2,1)S(1)}, u32[]{:S(2)}, u32[]{:S(2)}) async-start(bf16[32,64,128]{2,1,0:T(8,128)(2,1)} %bitcast.4), calls=%async_computation | async-start | bytes 1048576 | tf_op jit(solution)/shard_map/all_to_all | solution.py:70
  19.4 198.0 %all-gather.9.cloned.1.call-start = ((), (), s32[]{:S(2)}) async-start(), calls=%async_computation.3 | async-start | bytes 17301504 | tf_op jit(solution)/shard_map/all_gather | solution.py:100
  115.2 25.1 %copy-start.4 = (s32[256]{0:T(256)S(1)}, s32[256]{0:T(256)}, u32[]{:S(2)}) copy-start(s32[256]{0:T(256)} %param.19) | copy-start | bytes 3076
  139.5 0.8 copy-start.1
  394.7 128.1 %copy-start.3 = (f32[256]{0:T(256)S(1)}, f32[256]{0:T(256)}, u32[]{:S(2)}) copy-start(f32[256]{0:T(256)} %param.18) | copy-start | bytes 3076
  496.5 27.7 %copy-start = (bf16[2048,256]{1,0:T(8,128)(2,1)}, bf16[2048,256]{1,0:T(8,128)(2,1)S(1)}, u32[]{:S(2)}) copy-start(bf16[2048,256]{1,0:T(8,128)(2,1)S(1)} %get-tuple-element.207) | copy-start | bytes 3145732
Sparse Core Ops, SparseCore 0:
  10.5 52.7 all-gather.6
  65.9 47.9 all-gather.4
  140.4 76.9 all-gather.8
